TPU v7x, 32 devices: a whole 2x2x4 slice. The times are simulated.
32 devices in a mesh: groups: 2 (over y), section: 4 (over z), dp: 4 (over x, core).
Axes of the slice: x: 2, y: 2, z: 4, core: 2. Of those that a mesh axis runs over, the one named last changes fastest.
Arguments:
- stream_in: bfloat16 [1152, 3072], P(('groups', 'dp')), parts along dimension 0, may hold values from -6 to 6
- out_grad: bfloat16 [1152, 3072], P(('groups', 'dp')), parts along dimension 0, may hold values from -6 to 6
- mask_blocks: int32 [24, 3, 3], P(('groups', 'dp')), parts along dimension 0, may hold values from 0 to 2, as said below
- norm_gain: float32 [4, 3072], P('section'), may hold values from 0.4 to 1.6
- w_joined: bfloat16 [4, 3072, 1664], P('section', 'dp'), may hold values from -0.109375 to 0.109375
- w_out: bfloat16 [4, 1536, 3072], P('section', 'dp'), may hold values from -0.15625 to 0.15625
Outputs:
- grad_joined: float32 [8, 3072, 1664], P(('groups', 'section'), 'dp'), parts along dimension 0
- grad_out: float32 [8, 1536, 3072], P(('groups', 'section'), 'dp'), parts along dimension 0
- gain_grad: float32 [8, 3072], P(('groups', 'section')), parts along dimension 0
There are 2 independent parts, one for each index of `groups`. A program takes and returns all parts, laid end to end along the dimension named above; an argument that names none is the same for every part. Nothing has to cross between parts.
Inputs may be any that keep to these rules, and one draw needn't show every extreme that they name: `mask_blocks`: entry 0 of the list of query block i is i itself.
All inputs are finite; a program needn't handle non-finite values.
Results may differ from a plain program's by a relative error of at most 0.024.
Values may be sent and summed in bfloat16 or wider, within the bound.
A program may use at most 128 MiB of HBM per device.

v0:
```python
import jax
import jax.numpy as jnp
from jax import lax
from jax.sharding import PartitionSpec as P

NUM_HEADS = 24
HEAD_DIM = 64
BLOCK_LEN = 16
EPSILON = 1e-05


def from_behind(value, axis, steps):
    count = lax.axis_size(axis)
    initial, last = (max(0, -steps), min(count, count - steps))
    return lax.ppermute(value, axis, [(source, source + steps) for source in range(initial, last)])


def allowed_tokens(links, block_len):
    count = links.shape[1]
    block_hits = links[:, :, :, None] == jnp.arange(count, dtype=jnp.int32)[None, None, None, :]
    blocks = jnp.any(block_hits, axis=2)
    return jnp.repeat(jnp.repeat(blocks, block_len, axis=1), block_len, axis=2)


def normalize(stream, gain_row):
    stream_wide = stream.astype(jnp.float32)
    inv_rms = lax.rsqrt(jnp.mean(stream_wide * stream_wide, axis=-1, keepdims=True) + EPSILON)
    normed = (stream_wide * inv_rms * gain_row).astype(jnp.bfloat16)
    return (stream_wide, inv_rms, normed)


def project(normed, weight):
    batch_size, length, model_width = normed.shape
    flat = jnp.dot(normed.reshape(-1, model_width), weight, preferred_element_type=jnp.float32)
    return flat.astype(jnp.bfloat16).reshape(batch_size, length, weight.shape[1])


def attend(joined_rows, allowed):
    batch_size, length, _ = joined_rows.shape
    inner_width = NUM_HEADS * HEAD_DIM
    queries = joined_rows[:, :, :inner_width].reshape(batch_size, length, NUM_HEADS, HEAD_DIM)
    key_rows = joined_rows[:, :, inner_width : inner_width + HEAD_DIM]
    values = joined_rows[:, :, inner_width + HEAD_DIM :]
    scores = jnp.einsum(
        "bihd,bjd->bhij", queries, key_rows, preferred_element_type=jnp.float32
    ) * HEAD_DIM ** (-0.5)
    scores = jnp.where(allowed[:, None], scores, -1e30)
    row_max = jnp.max(scores, axis=-1, keepdims=True)
    exp_scores = jnp.exp(scores - row_max)
    attn_probs = exp_scores / jnp.sum(exp_scores, axis=-1, keepdims=True)
    probs_half = attn_probs.astype(jnp.bfloat16)
    mixed_heads = jnp.einsum(
        "bhij,bjd->bihd", probs_half, values, preferred_element_type=jnp.float32
    )
    mixed_heads = mixed_heads.astype(jnp.bfloat16).reshape(batch_size, length, inner_width)
    return (queries, key_rows, values, attn_probs, probs_half, mixed_heads)


def layer_forward(stream, gain_row, w_joined, w_out, allowed):
    stream_wide, inv_rms, normed = normalize(stream, gain_row)
    joined_rows = project(normed, w_joined)
    mixed_heads = attend(joined_rows, allowed)[5]
    batch_size, length, model_width = stream.shape
    update = jnp.dot(
        mixed_heads.reshape(-1, mixed_heads.shape[2]), w_out, preferred_element_type=jnp.float32
    )
    result = (stream_wide + update.reshape(batch_size, length, model_width)).astype(jnp.bfloat16)
    return (result, joined_rows)


def layer_backward(stream, gain_row, joined_rows, w_joined, w_out, allowed, upstream):
    stream_wide, inv_rms, normed = normalize(stream, gain_row)
    queries, key_rows, values, attn_probs, probs_half, mixed_heads = attend(joined_rows, allowed)
    batch_size, length, model_width = stream.shape
    inner_width = NUM_HEADS * HEAD_DIM
    grad_mixed = lax.dot_general(
        upstream.reshape(-1, model_width),
        w_out,
        (((1,), (1,)), ((), ())),
        preferred_element_type=jnp.float32,
    )
    grad_mixed = grad_mixed.astype(jnp.bfloat16).reshape(batch_size, length, NUM_HEADS, HEAD_DIM)
    grad_probs = jnp.einsum(
        "bihd,bjd->bhij", grad_mixed, values, preferred_element_type=jnp.float32
    )
    grad_values = jnp.einsum(
        "bhij,bihd->bjd", probs_half, grad_mixed, preferred_element_type=jnp.float32
    )
    inner_sum = jnp.sum(attn_probs * grad_probs, axis=-1, keepdims=True)
    grad_scores = (attn_probs * (grad_probs - inner_sum) * HEAD_DIM ** (-0.5)).astype(jnp.bfloat16)
    grad_queries = jnp.einsum(
        "bhij,bjd->bihd", grad_scores, key_rows, preferred_element_type=jnp.float32
    )
    grad_keys = jnp.einsum(
        "bhij,bihd->bjd", grad_scores, queries, preferred_element_type=jnp.float32
    )
    grad_joined_rows = jnp.concatenate(
        [grad_queries.reshape(batch_size, length, inner_width), grad_keys, grad_values], axis=-1
    ).astype(jnp.bfloat16)
    grad_normed = lax.dot_general(
        grad_joined_rows.reshape(-1, grad_joined_rows.shape[2]),
        w_joined,
        (((1,), (1,)), ((), ())),
        preferred_element_type=jnp.float32,
    )
    grad_normed = grad_normed.reshape(batch_size, length, model_width)
    gained = grad_normed * gain_row
    grad_stream = inv_rms * gained - stream_wide * inv_rms**3 * jnp.mean(
        stream_wide * gained, axis=-1, keepdims=True
    )
    down_grad = (upstream.astype(jnp.float32) + grad_stream).astype(jnp.bfloat16)
    gain_part = jnp.sum((grad_normed * stream_wide * inv_rms).reshape(-1, model_width), axis=0)
    return (down_grad, normed, grad_joined_rows, mixed_heads, gain_part)


def pass_forward(values):
    return from_behind(values, "section", 1)


def pass_backward(values):
    return from_behind(values, "section", -1)


def body(stream_in, out_grad, mask_blocks, norm_gain, w_joined, w_out):
    gathered = (
        lax.all_gather(w_joined, "dp", axis=1, tiled=True),
        lax.all_gather(w_out, "dp", axis=1, tiled=True),
    )
    full_joined = gathered[0][0]
    full_out = gathered[1][0]
    gain_row = norm_gain[0]
    sections = lax.axis_size("section")
    section_index = lax.axis_index("section")
    micro_count = mask_blocks.shape[0]
    model_width = stream_in.shape[1]
    length = stream_in.shape[0] // micro_count
    joined_width = full_joined.shape[1]
    inner_width = full_out.shape[0]
    per_group = micro_count // micro_count
    inputs = stream_in.reshape(micro_count, per_group, length, model_width)
    upstreams = out_grad.reshape(micro_count, per_group, length, model_width)
    allowed = allowed_tokens(mask_blocks, BLOCK_LEN).reshape(micro_count, per_group, length, length)
    step_count = micro_count + sections - 1
    keep_shape = (1,)

    def forward_step(step_now, state_now):
        incoming, kept_inputs, kept_joined = state_now
        slot_index = step_now - section_index
        active = jnp.logical_and(slot_index >= 0, slot_index < micro_count)
        group_index = jnp.clip(slot_index, 0, micro_count - 1)
        source = jnp.where(section_index == 0, inputs[group_index], incoming)

        def forward_run(kept_pair):
            result, joined_rows = layer_forward(
                source, gain_row, full_joined, full_out, allowed[group_index]
            )
            new_inputs = lax.dynamic_update_index_in_dim(kept_pair[0], source, group_index, 0)
            new_joined = kept_pair[1]
            return (result, new_inputs, new_joined)

        def forward_rest(kept_pair):
            return (jnp.zeros_like(source), kept_pair[0], kept_pair[1])

        result, kept_inputs, kept_joined = lax.cond(
            active, forward_run, forward_rest, (kept_inputs, kept_joined)
        )
        return (pass_forward(result), kept_inputs, kept_joined)

    start_state = (
        jnp.zeros((per_group, length, model_width), jnp.bfloat16),
        jnp.zeros((micro_count, per_group, length, model_width), jnp.bfloat16),
        jnp.zeros(keep_shape, jnp.bfloat16),
    )
    _, kept_inputs, kept_joined = lax.fori_loop(0, step_count, forward_step, start_state)

    def backward_step(step_now, state_now):
        incoming, stores = state_now
        slot_index = step_now - (sections - 1 - section_index)
        active = jnp.logical_and(slot_index >= 0, slot_index < micro_count)
        group_index = jnp.clip(slot_index, 0, micro_count - 1)
        upstream = jnp.where(section_index == sections - 1, upstreams[group_index], incoming)

        def backward_run(store_now):
            source = kept_inputs[group_index]
            joined_rows = project(normalize(source, gain_row)[2], full_joined)
            down_grad, normed, grad_joined_rows, mixed_heads, gain_part = layer_backward(
                source, gain_row, joined_rows, full_joined, full_out, allowed[group_index], upstream
            )
            new_store = (
                lax.dynamic_update_index_in_dim(store_now[0], normed, group_index, 0),
                lax.dynamic_update_index_in_dim(store_now[1], grad_joined_rows, group_index, 0),
                lax.dynamic_update_index_in_dim(store_now[2], mixed_heads, group_index, 0),
                lax.dynamic_update_index_in_dim(store_now[3], upstream, group_index, 0),
                store_now[4] + gain_part,
            )
            return (down_grad, new_store)

        def backward_rest(store_now):
            return (jnp.zeros_like(upstream), store_now)

        down_grad, stores = lax.cond(active, backward_run, backward_rest, stores)
        return (pass_backward(down_grad), stores)

    empty_stores = (
        jnp.zeros((micro_count, per_group, length, model_width), jnp.bfloat16),
        jnp.zeros((micro_count, per_group, length, joined_width), jnp.bfloat16),
        jnp.zeros((micro_count, per_group, length, inner_width), jnp.bfloat16),
        jnp.zeros((micro_count, per_group, length, model_width), jnp.bfloat16),
        jnp.zeros((model_width,), jnp.float32),
    )
    start_back = (jnp.zeros((per_group, length, model_width), jnp.bfloat16), empty_stores)
    _, stores = lax.fori_loop(0, step_count, backward_step, start_back)
    rows_normed = stores[0].reshape(-1, model_width)
    rows_joined = stores[1].reshape(-1, joined_width)
    rows_mixed = stores[2].reshape(-1, inner_width)
    rows_upstream = stores[3].reshape(-1, model_width)
    columns = rows_normed
    grad_joined = lax.psum_scatter(
        lax.dot_general(
            columns, rows_joined, (((0,), (0,)), ((), ())), preferred_element_type=jnp.float32
        ).astype(jnp.bfloat16),
        "dp",
        scatter_dimension=0,
        tiled=True,
    ).astype(jnp.float32)
    columns = rows_mixed
    grad_output = lax.psum_scatter(
        lax.dot_general(
            columns, rows_upstream, (((0,), (0,)), ((), ())), preferred_element_type=jnp.float32
        ).astype(jnp.bfloat16),
        "dp",
        scatter_dimension=0,
        tiled=True,
    ).astype(jnp.float32)
    gain_total = lax.psum(stores[4], "dp")
    return (grad_joined[None], grad_output[None], gain_total[None])


def solution(mesh):
    return jax.shard_map(
        body,
        mesh=mesh,
        in_specs=(
            P(("groups", "dp"), None),
            P(("groups", "dp"), None),
            P(("groups", "dp"), None, None),
            P("section", None),
            P("section", "dp", None),
            P("section", "dp", None),
        ),
        out_specs=(
            P(("groups", "section"), "dp", None),
            P(("groups", "section"), "dp", None),
            P(("groups", "section"), None),
        ),
        check_vma=False,
    )
```

profile of v0, /device:TPU:0, one launch (start us, length us, event | category | flops | bytes accessed | tf_op | source)
XLA Modules:
  0.0 678.1 jit_solution(13582287614701834989)
XLA Ops:
  9.8 66.7 %all-gather.5.cloned.1.call-done = bf16[1,1536,3072]{2,1,0:T(8,128)(2,1)} async-done(((bf16[1,384,3072]{2,1,0:T(8,128)(2,1)}), bf16[1,1536,3072]{2,1,0:T(8,128)(2,1)}) %all-gather.5.cloned.1.call-update) | async-done | bytes 9437200 | tf_op jit(solution)/shard_map/all_gather | solution.py:127
  76.5 70.3 %all-gather.3.cloned.1.call-done = bf16[1,3072,1664]{2,1,0:T(8,128)(2,1)} async-done(((bf16[1,768,1664]{2,1,0:T(8,128)(2,1)}), bf16[1,3072,1664]{2,1,0:T(8,128)(2,1)}) %all-gather.3.cloned.1.call-update) | async-done | bytes 10223632 | tf_op jit(solution)/shard_map/all_gather | solution.py:126
  146.9 123.2 %while.46 = (s32[]{:T(128)}, bf16[1,48,3072]{2,1,0:T(8,128)(2,1)S(1)}, bf16[3,1,48,3072]{3,2,1,0:T(8,128)(2,1)S(1)}, s32[]{:T(128)}, pred[]{:T(512)}, /*index=5*...) while((s32[]{:T(128)}, ...), condition=%wide.region_7.8_spmd.clone, body=%wide.region_1.7_spmd.clone.sunk | while | flops 960089920 | bytes 26255604 | solution.py:174
  147.0 14.0 %conditional.6 = (bf16[1,48,3072]{2,1,0:T(8,128)(2,1)S(1)}, bf16[3,1,48,3072]{3,2,1,0:T(8,128)(2,1)S(1)}) conditional(s32[]{:T(128)} %convert_element_type.279, bf16[3,1,48,3072]{3,2,1,0:T(8,128)(2,1)S(1)} %get-tuple-element.1143, (pred[]{:T(512)}, s32[]{:T(128)}, bf16[3,1,48,3072]{3,2,1,0:T(8,128)(2,1)}, bf16[1,48,3072]{2,1,0:T(8,128)(2,1)S(1)}, ...), branch_computations={%region_2.2_spmd, %region_3.6_spmd} | conditional | flops 960089920 | bytes 25068336 | solution.py:164
  169.3 14.0 %conditional.6 = (bf16[1,48,3072]{2,1,0:T(8,128)(2,1)S(1)}, bf16[3,1,48,3072]{3,2,1,0:T(8,128)(2,1)S(1)}) conditional(s32[]{:T(128)} %convert_element_type.279, bf16[3,1,48,3072]{3,2,1,0:T(8,128)(2,1)S(1)} %get-tuple-element.1143, (pred[]{:T(512)}, s32[]{:T(128)}, bf16[3,1,48,3072]{3,2,1,0:T(8,128)(2,1)}, bf16[1,48,3072]{2,1,0:T(8,128)(2,1)S(1)}, ...), branch_computations={%region_2.2_spmd, %region_3.6_spmd} | conditional | flops 960089920 | bytes 25068336 | solution.py:164
  193.9 14.0 %conditional.6 = (bf16[1,48,3072]{2,1,0:T(8,128)(2,1)S(1)}, bf16[3,1,48,3072]{3,2,1,0:T(8,128)(2,1)S(1)}) conditional(s32[]{:T(128)} %convert_element_type.279, bf16[3,1,48,3072]{3,2,1,0:T(8,128)(2,1)S(1)} %get-tuple-element.1143, (pred[]{:T(512)}, s32[]{:T(128)}, bf16[3,1,48,3072]{3,2,1,0:T(8,128)(2,1)}, bf16[1,48,3072]{2,1,0:T(8,128)(2,1)S(1)}, ...), branch_computations={%region_2.2_spmd, %region_3.6_spmd} | conditional | flops 960089920 | bytes 25068336 | solution.py:164
  217.6 18.4 %collective-permute-start = (bf16[1,48,3072]{2,1,0:T(8,128)(2,1)S(1)}, bf16[1,48,3072]{2,1,0:T(8,128)(2,1)S(1)}, u32[]{:S(2)}, u32[]{:S(2)}) collective-permute-start(bf16[1,48,3072]{2,1,0:T(8,128)(2,1)S(1)} %get-tuple-element.1089), channel_id=1, source_target_pairs={{0,4},{4,8},{8,12},{1,5},{5,9},{9,13},{2,6},{6,10},{10,14},{3,7},{... | collective-permute-start | bytes 884744 | tf_op jit(solution)/shard_map/while/body/eval_jaxpr/ppermute | solution.py:15
  249.1 16.8 %collective-permute-start = (bf16[1,48,3072]{2,1,0:T(8,128)(2,1)S(1)}, bf16[1,48,3072]{2,1,0:T(8,128)(2,1)S(1)}, u32[]{:S(2)}, u32[]{:S(2)}) collective-permute-start(bf16[1,48,3072]{2,1,0:T(8,128)(2,1)S(1)} %get-tuple-element.1089), channel_id=1, source_target_pairs={{0,4},{4,8},{8,12},{1,5},{5,9},{9,13},{2,6},{6,10},{10,14},{3,7},{... | collective-permute-start | bytes 884744 | tf_op jit(solution)/shard_map/while/body/eval_jaxpr/ppermute | solution.py:15
  273.0 224.6 %while.47 = (s32[]{:T(128)}, bf16[1,48,3072]{2,1,0:T(8,128)(2,1)S(1)}, bf16[3,1,48,3072]{3,2,1,0:T(8,128)(2,1)}, bf16[3,1,48,1664]{3,2,1,0:T(8,128)(2,1)S(1)}, b...) while((s32[]{:T(128)}, ...), condition=%wide.region_17.18_spmd.clone, body=%wide.region_8.17_spmd.clone.sunk | while | flops 1482513152 | bytes 44681152 | solution.py:212
  274.4 7.8 %collective-permute-done.1 = bf16[1,48,3072]{2,1,0:T(8,128)(2,1)S(1)} collective-permute-done((bf16[1,48,3072]{2,1,0:T(8,128)(2,1)S(1)}, bf16[1,48,3072]{2,1,0:T(8,128)(2,1)S(1)}, u32[]{:S(2)}, u32[]{:S(2)}) %collective-permute-start.1) | collective-permute-done | bytes 294944 | tf_op jit(solution)/shard_map/while/body/eval_jaxpr/ppermute | solution.py:15
  283.5 19.8 %collective-permute-done.1 = bf16[1,48,3072]{2,1,0:T(8,128)(2,1)S(1)} collective-permute-done((bf16[1,48,3072]{2,1,0:T(8,128)(2,1)S(1)}, bf16[1,48,3072]{2,1,0:T(8,128)(2,1)S(1)}, u32[]{:S(2)}, u32[]{:S(2)}) %collective-permute-start.1) | collective-permute-done | bytes 294944 | tf_op jit(solution)/shard_map/while/body/eval_jaxpr/ppermute | solution.py:15
  304.7 87.0 %collective-permute-done.1 = bf16[1,48,3072]{2,1,0:T(8,128)(2,1)S(1)} collective-permute-done((bf16[1,48,3072]{2,1,0:T(8,128)(2,1)S(1)}, bf16[1,48,3072]{2,1,0:T(8,128)(2,1)S(1)}, u32[]{:S(2)}, u32[]{:S(2)}) %collective-permute-start.1) | collective-permute-done | bytes 294944 | tf_op jit(solution)/shard_map/while/body/eval_jaxpr/ppermute | solution.py:15
  391.7 26.7 %conditional.7 = (bf16[1,48,3072]{2,1,0:T(8,128)(2,1)S(1)}, bf16[3,1,48,3072]{3,2,1,0:T(8,128)(2,1)}, bf16[3,1,48,1664]{3,2,1,0:T(8,128)(2,1)S(1)}, bf16[3,1,48,...) conditional(s32[]{:T(128)} %convert_element_type.280, ...), branch_computations={%region_9.9_spmd, %region_10.16_spmd} | conditional | flops 1482513152 | bytes 43493764 | solution.py:201
  410.8 7.2 %fusion.40 = (f32[3072]{0:T(1024)S(1)}, f32[48]{0:T(128)S(1)}, f32[48,3072]{1,0:T(8,128)S(1)}) fusion(f32[48]{0:T(128)S(1)} %get-tuple-element.937, bf16[3,1,48,3072]{3,2,1,0:T(8,128)(2,1)S(1)} %get-tuple-element.767, s32[]{:T(128)S(6)} %min.21, f32[3072]{0:T(1024)S(1)} %bitcast.198, bf16[48,1664]{1,0:T(8,128)(2,1)S(1)} %concatenate.26, ...), kind=kOutput, calls=%fused_computation.62 | convolution fusion | flops 491762624 | bytes 11293060 | tf_op jit(solution)/shard_map/while/body/eval_jaxpr/cond/branch_1_fun/dot_general | solution.py:100
  419.7 7.3 %collective-permute-done.1 = bf16[1,48,3072]{2,1,0:T(8,128)(2,1)S(1)} collective-permute-done((bf16[1,48,3072]{2,1,0:T(8,128)(2,1)S(1)}, bf16[1,48,3072]{2,1,0:T(8,128)(2,1)S(1)}, u32[]{:S(2)}, u32[]{:S(2)}) %collective-permute-start.1) | collective-permute-done | bytes 294944 | tf_op jit(solution)/shard_map/while/body/eval_jaxpr/ppermute | solution.py:15
  427.0 26.7 %conditional.7 = (bf16[1,48,3072]{2,1,0:T(8,128)(2,1)S(1)}, bf16[3,1,48,3072]{3,2,1,0:T(8,128)(2,1)}, bf16[3,1,48,1664]{3,2,1,0:T(8,128)(2,1)S(1)}, bf16[3,1,48,...) conditional(s32[]{:T(128)} %convert_element_type.280, ...), branch_computations={%region_9.9_spmd, %region_10.16_spmd} | conditional | flops 1482513152 | bytes 43493764 | solution.py:201
  455.0 7.3 %collective-permute-done.1 = bf16[1,48,3072]{2,1,0:T(8,128)(2,1)S(1)} collective-permute-done((bf16[1,48,3072]{2,1,0:T(8,128)(2,1)S(1)}, bf16[1,48,3072]{2,1,0:T(8,128)(2,1)S(1)}, u32[]{:S(2)}, u32[]{:S(2)}) %collective-permute-start.1) | collective-permute-done | bytes 294944 | tf_op jit(solution)/shard_map/while/body/eval_jaxpr/ppermute | solution.py:15
  462.3 26.7 %conditional.7 = (bf16[1,48,3072]{2,1,0:T(8,128)(2,1)S(1)}, bf16[3,1,48,3072]{3,2,1,0:T(8,128)(2,1)}, bf16[3,1,48,1664]{3,2,1,0:T(8,128)(2,1)S(1)}, bf16[3,1,48,...) conditional(s32[]{:T(128)} %convert_element_type.280, ...), branch_computations={%region_9.9_spmd, %region_10.16_spmd} | conditional | flops 1482513152 | bytes 43493764 | solution.py:201
  490.3 7.3 %collective-permute-done.1 = bf16[1,48,3072]{2,1,0:T(8,128)(2,1)S(1)} collective-permute-done((bf16[1,48,3072]{2,1,0:T(8,128)(2,1)S(1)}, bf16[1,48,3072]{2,1,0:T(8,128)(2,1)S(1)}, u32[]{:S(2)}, u32[]{:S(2)}) %collective-permute-start.1) | collective-permute-done | bytes 294944 | tf_op jit(solution)/shard_map/while/body/eval_jaxpr/ppermute | solution.py:15
  497.6 7.6 %bitcast_convert_fusion.1 = bf16[1536,3072]{1,0:T(8,128)(2,1)} fusion(bf16[3,1,48,3072]{3,2,1,0:T(8,128)(2,1)} %get-tuple-element.812, bf16[3,1,48,1536]{3,2,1,0:T(8,128)(2,1)} %get-tuple-element.811), kind=kOutput, calls=%fused_computation.97 | convolution fusion | flops 1363673088 | bytes 10764288 | tf_op jit(solution)/shard_map/dot_general | solution.py:228
  505.5 10.6 %bitcast_convert_fusion = bf16[3072,1664]{1,0:T(8,128)(2,1)} fusion(bf16[3,1,48,3072]{3,2,1,0:T(8,128)(2,1)} %get-tuple-element.809, bf16[3,1,48,1664]{3,2,1,0:T(8,128)(2,1)S(1)} %get-tuple-element.810), kind=kOutput, calls=%fused_computation.96 | convolution fusion | flops 1477312512 | bytes 11587584 | tf_op jit(solution)/shard_map/dot_general | solution.py:219
  516.2 10.7 %psum.7 = f32[1,3072]{1,0:T(1,128)} all-reduce(f32[1,3072]{1,0:T(1,128)S(1)} %bitcast.206), channel_id=1, replica_groups=mesh['groups'=2,'section'=4,'dp'=4] {'dp'}, use_global_device_ids=true, to_apply=%region_20.21 | all-reduce | flops 3072 | bytes 24576 | tf_op jit(solution)/shard_map/psum | solution.py:235
  526.9 54.2 %reduce-scatter.5.cloned.1.call-done = bf16[384,3072]{1,0:T(8,128)(2,1)} async-done(((bf16[1536,3072]{1,0:T(8,128)(2,1)}), bf16[384,3072]{1,0:T(8,128)(2,1)}) %reduce-scatter.5.cloned.1.call-update) | async-done | bytes 2359312 | tf_op jit(solution)/shard_map/reduce_scatter | solution.py:227
  585.5 81.7 %reduce-scatter.3.cloned.1.call-done = bf16[768,1664]{1,0:T(8,128)(2,1)} async-done(((bf16[3072,1664]{1,0:T(8,128)(2,1)}), bf16[768,1664]{1,0:T(8,128)(2,1)}) %reduce-scatter.3.cloned.1.call-update) | async-done | bytes 2555920 | tf_op jit(solution)/shard_map/reduce_scatter | solution.py:218
  (196 shorter events, 182.5 us)
Async XLA Ops:
  7.2 69.4 %all-gather.5.cloned.1.call-start = ((), (), s32[]{:S(2)}) async-start(), calls=%async_computation.3 | async-start | bytes 11796480 | tf_op jit(solution)/shard_map/all_gather | solution.py:127
  7.9 138.9 %all-gather.3.cloned.1.call-start = ((), (), s32[]{:S(2)}) async-start(), calls=%async_computation.2 | async-start | bytes 12779520 | tf_op jit(solution)/shard_map/all_gather | solution.py:126
  8.6 572.5 %reduce-scatter.5.cloned.1.call-start = ((), (), s32[]{:S(2)}) async-start(), calls=%async_computation.5 | async-start | bytes 11796480 | tf_op jit(solution)/shard_map/reduce_scatter | solution.py:227
  161.0 8.3 %collective-permute-start = (bf16[1,48,3072]{2,1,0:T(8,128)(2,1)S(1)}, bf16[1,48,3072]{2,1,0:T(8,128)(2,1)S(1)}, u32[]{:S(2)}, u32[]{:S(2)}) collective-permute-start(bf16[1,48,3072]{2,1,0:T(8,128)(2,1)S(1)} %get-tuple-element.1089), channel_id=1, source_target_pairs={{0,4},{4,8},{8,12},{1,5},{5,9},{9,13},{2,6},{6,10},{10,14},{3,7},{... | collective-permute-start | bytes 884744 | tf_op jit(solution)/shard_map/while/body/eval_jaxpr/ppermute | solution.py:15
  183.3 10.6 %collective-permute-start = (bf16[1,48,3072]{2,1,0:T(8,128)(2,1)S(1)}, bf16[1,48,3072]{2,1,0:T(8,128)(2,1)S(1)}, u32[]{:S(2)}, u32[]{:S(2)}) collective-permute-start(bf16[1,48,3072]{2,1,0:T(8,128)(2,1)S(1)} %get-tuple-element.1089), channel_id=1, source_target_pairs={{0,4},{4,8},{8,12},{1,5},{5,9},{9,13},{2,6},{6,10},{10,14},{3,7},{... | collective-permute-start | bytes 884744 | tf_op jit(solution)/shard_map/while/body/eval_jaxpr/ppermute | solution.py:15
  207.9 9.7 %collective-permute-start = (bf16[1,48,3072]{2,1,0:T(8,128)(2,1)S(1)}, bf16[1,48,3072]{2,1,0:T(8,128)(2,1)S(1)}, u32[]{:S(2)}, u32[]{:S(2)}) collective-permute-start(bf16[1,48,3072]{2,1,0:T(8,128)(2,1)S(1)} %get-tuple-element.1089), channel_id=1, source_target_pairs={{0,4},{4,8},{8,12},{1,5},{5,9},{9,13},{2,6},{6,10},{10,14},{3,7},{... | collective-permute-start | bytes 884744 | tf_op jit(solution)/shard_map/while/body/eval_jaxpr/ppermute | solution.py:15
  217.6 22.7 %collective-permute-start = (bf16[1,48,3072]{2,1,0:T(8,128)(2,1)S(1)}, bf16[1,48,3072]{2,1,0:T(8,128)(2,1)S(1)}, u32[]{:S(2)}, u32[]{:S(2)}) collective-permute-start(bf16[1,48,3072]{2,1,0:T(8,128)(2,1)S(1)} %get-tuple-element.1089), channel_id=1, source_target_pairs={{0,4},{4,8},{8,12},{1,5},{5,9},{9,13},{2,6},{6,10},{10,14},{3,7},{... | collective-permute-start | bytes 884744 | tf_op jit(solution)/shard_map/while/body/eval_jaxpr/ppermute | solution.py:15
  240.4 8.6 %collective-permute-start = (bf16[1,48,3072]{2,1,0:T(8,128)(2,1)S(1)}, bf16[1,48,3072]{2,1,0:T(8,128)(2,1)S(1)}, u32[]{:S(2)}, u32[]{:S(2)}) collective-permute-start(bf16[1,48,3072]{2,1,0:T(8,128)(2,1)S(1)} %get-tuple-element.1089), channel_id=1, source_target_pairs={{0,4},{4,8},{8,12},{1,5},{5,9},{9,13},{2,6},{6,10},{10,14},{3,7},{... | collective-permute-start | bytes 884744 | tf_op jit(solution)/shard_map/while/body/eval_jaxpr/ppermute | solution.py:15
  249.1 21.0 %collective-permute-start = (bf16[1,48,3072]{2,1,0:T(8,128)(2,1)S(1)}, bf16[1,48,3072]{2,1,0:T(8,128)(2,1)S(1)}, u32[]{:S(2)}, u32[]{:S(2)}) collective-permute-start(bf16[1,48,3072]{2,1,0:T(8,128)(2,1)S(1)} %get-tuple-element.1089), channel_id=1, source_target_pairs={{0,4},{4,8},{8,12},{1,5},{5,9},{9,13},{2,6},{6,10},{10,14},{3,7},{... | collective-permute-start | bytes 884744 | tf_op jit(solution)/shard_map/while/body/eval_jaxpr/ppermute | solution.py:15
  273.1 9.1 %collective-permute-start.1 = (bf16[1,48,3072]{2,1,0:T(8,128)(2,1)S(1)}, bf16[1,48,3072]{2,1,0:T(8,128)(2,1)S(1)}, u32[]{:S(2)}, u32[]{:S(2)}) collective-permute-start(bf16[1,48,3072]{2,1,0:T(8,128)(2,1)S(1)} %get-tuple-element.1106), channel_id=1, source_target_pairs={{4,0},{8,4},{12,8},{5,1},{9,5},{13,9},{6,2},{10,6},{14,10},{7,3},{... | collective-permute-start | bytes 884744 | tf_op jit(solution)/shard_map/while/body/eval_jaxpr/ppermute | solution.py:15
  282.2 21.1 %collective-permute-start.1 = (bf16[1,48,3072]{2,1,0:T(8,128)(2,1)S(1)}, bf16[1,48,3072]{2,1,0:T(8,128)(2,1)S(1)}, u32[]{:S(2)}, u32[]{:S(2)}) collective-permute-start(bf16[1,48,3072]{2,1,0:T(8,128)(2,1)S(1)} %get-tuple-element.1106), channel_id=1, source_target_pairs={{4,0},{8,4},{12,8},{5,1},{9,5},{13,9},{6,2},{10,6},{14,10},{7,3},{... | collective-permute-start | bytes 884744 | tf_op jit(solution)/shard_map/while/body/eval_jaxpr/ppermute | solution.py:15
  303.4 88.3 %collective-permute-start.1 = (bf16[1,48,3072]{2,1,0:T(8,128)(2,1)S(1)}, bf16[1,48,3072]{2,1,0:T(8,128)(2,1)S(1)}, u32[]{:S(2)}, u32[]{:S(2)}) collective-permute-start(bf16[1,48,3072]{2,1,0:T(8,128)(2,1)S(1)} %get-tuple-element.1106), channel_id=1, source_target_pairs={{4,0},{8,4},{12,8},{5,1},{9,5},{13,9},{6,2},{10,6},{14,10},{7,3},{... | collective-permute-start | bytes 884744 | tf_op jit(solution)/shard_map/while/body/eval_jaxpr/ppermute | solution.py:15
  391.9 8.0 %copy-start = (f32[1,3072]{1,0:T(1,128)S(1)}, f32[1,3072]{1,0:T(1,128)}, u32[]{:S(2)}) copy-start(f32[1,3072]{1,0:T(1,128)} %get-tuple-element.768) | copy-start | bytes 36868 | tf_op jit(solution)/shard_map/while/body/eval_jaxpr/cond
  418.4 8.6 %collective-permute-start.1 = (bf16[1,48,3072]{2,1,0:T(8,128)(2,1)S(1)}, bf16[1,48,3072]{2,1,0:T(8,128)(2,1)S(1)}, u32[]{:S(2)}, u32[]{:S(2)}) collective-permute-start(bf16[1,48,3072]{2,1,0:T(8,128)(2,1)S(1)} %get-tuple-element.1106), channel_id=1, source_target_pairs={{4,0},{8,4},{12,8},{5,1},{9,5},{13,9},{6,2},{10,6},{14,10},{7,3},{... | collective-permute-start | bytes 884744 | tf_op jit(solution)/shard_map/while/body/eval_jaxpr/ppermute | solution.py:15
  427.3 8.0 %copy-start = (f32[1,3072]{1,0:T(1,128)S(1)}, f32[1,3072]{1,0:T(1,128)}, u32[]{:S(2)}) copy-start(f32[1,3072]{1,0:T(1,128)} %get-tuple-element.768) | copy-start | bytes 36868 | tf_op jit(solution)/shard_map/while/body/eval_jaxpr/cond
  453.7 8.6 %collective-permute-start.1 = (bf16[1,48,3072]{2,1,0:T(8,128)(2,1)S(1)}, bf16[1,48,3072]{2,1,0:T(8,128)(2,1)S(1)}, u32[]{:S(2)}, u32[]{:S(2)}) collective-permute-start(bf16[1,48,3072]{2,1,0:T(8,128)(2,1)S(1)} %get-tuple-element.1106), channel_id=1, source_target_pairs={{4,0},{8,4},{12,8},{5,1},{9,5},{13,9},{6,2},{10,6},{14,10},{7,3},{... | collective-permute-start | bytes 884744 | tf_op jit(solution)/shard_map/while/body/eval_jaxpr/ppermute | solution.py:15
  462.6 8.0 %copy-start = (f32[1,3072]{1,0:T(1,128)S(1)}, f32[1,3072]{1,0:T(1,128)}, u32[]{:S(2)}) copy-start(f32[1,3072]{1,0:T(1,128)} %get-tuple-element.768) | copy-start | bytes 36868 | tf_op jit(solution)/shard_map/while/body/eval_jaxpr/cond
  489.0 8.6 %collective-permute-start.1 = (bf16[1,48,3072]{2,1,0:T(8,128)(2,1)S(1)}, bf16[1,48,3072]{2,1,0:T(8,128)(2,1)S(1)}, u32[]{:S(2)}, u32[]{:S(2)}) collective-permute-start(bf16[1,48,3072]{2,1,0:T(8,128)(2,1)S(1)} %get-tuple-element.1106), channel_id=1, source_target_pairs={{4,0},{8,4},{12,8},{5,1},{9,5},{13,9},{6,2},{10,6},{14,10},{7,3},{... | collective-permute-start | bytes 884744 | tf_op jit(solution)/shard_map/while/body/eval_jaxpr/ppermute | solution.py:15
  505.3 162.0 %reduce-scatter.3.cloned.1.call-start = ((), (), s32[]{:S(2)}) async-start(), calls=%async_computation.4 | async-start | bytes 12779520 | tf_op jit(solution)/shard_map/reduce_scatter | solution.py:218
Sparse Core Ops, SparseCore 0:
  9.6 66.9 all-gather.4
  78.1 68.6 all-gather.2
  505.4 75.6 reduce-scatter.4
  583.6 83.6 reduce-scatter.2
where the time goes:
time: 679 us; the launch traced here: 678 us
  waiting for transfers between devices  442 us (65%)
  matrix products  120 us (18%)
  starting transfers between devices  57.8 us (9%)
  other arithmetic  21.6 us (3%)
  between operations  13.8 us (2%)
  local copies, waits for them, and re-layouts  11.3 us (2%)
  blocking collectives  10.7 us (2%)
    ppermute x12, waiting for transfers between devices, from_behind(): lax.ppermute(value, axis, [(source, source + steps) for source in range(i...  168 us
    reduce_scatter x1, waiting for transfers between devices, body(): lax.psum_scatter(lax.dot_general(columns, rows_joined, (((0,), (0,)), (()...  81.7 us
    all_gather x1, waiting for transfers between devices, body(): lax.all_gather(w_joined, 'dp', axis=1, tiled=True)  70.3 us
    all_gather x1, waiting for transfers between devices, body(): lax.all_gather(w_out, 'dp', axis=1, tiled=True)  66.7 us
    ppermute x12, starting transfers between devices, from_behind(): lax.ppermute(value, axis, [(source, source + steps) for source in range(i...  57.4 us
    reduce_scatter x1, waiting for transfers between devices, body(): lax.psum_scatter(lax.dot_general(columns, rows_upstream, (((0,), (0,)), (...  54.2 us
    dot_general x6, matrix products, project(): jnp.dot(normed.reshape(-1, model_width), weight, preferred_element_type=j...  35.1 us
    dot_general x3, matrix products, layer_backward(): lax.dot_general(grad_joined_rows.reshape(-1, grad_joined_rows.shape[2]),...  21.5 us
  transfers between devices with their start and end apart: 16, of which 16 were waited for; matrix products, arithmetic and copies ran while one was open for 2% of the time, Pallas kernels for 0%

commit v1 on v0

--- a/solution.py
+++ b/solution.py
@@ -7,6 +7,18 @@
 HEAD_DIM = 64
 BLOCK_LEN = 16
 EPSILON = 1e-05
+
+
+def gather_by_bits(x, axis, dim):
+    ways, here, step = (lax.axis_size(axis), lax.axis_index(axis), x.shape[dim])
+    line, have = (x, 1)
+    while have < ways:
+        line = jnp.concatenate(
+            [line, lax.ppermute(line, axis, [(d, (d - have) % ways) for d in range(ways)])],
+            axis=dim,
+        )
+        have = 2 * have
+    return jnp.roll(line, here * step, axis=dim)
 
 
 def from_behind(value, axis, steps):
@@ -122,10 +134,7 @@
 
 
 def body(stream_in, out_grad, mask_blocks, norm_gain, w_joined, w_out):
-    gathered = (
-        lax.all_gather(w_joined, "dp", axis=1, tiled=True),
-        lax.all_gather(w_out, "dp", axis=1, tiled=True),
-    )
+    gathered = (gather_by_bits(w_joined, "dp", 1), lax.all_gather(w_out, "dp", axis=1, tiled=True))
     full_joined = gathered[0][0]
     full_out = gathered[1][0]
     gain_row = norm_gain[0]

time: 679 us -> 763 us (1.12)
  waiting for transfers between devices: 442 us -> 486 us
  local copies, waits for them, and re-layouts: 11.3 us -> 44.6 us
    ppermute x0 -> x2, waiting for transfers between devices: none -> 178 us  [gather_by_bits(): lax.ppermute(line, axis, [(d, (d - have) % ways) for d in range(ways)])]
    all_gather x1 -> x0, waiting for transfers between devices: 70.3 us -> none  [body(): lax.all_gather(w_joined, 'dp', axis=1, tiled=True)]
    all_gather x1, waiting for transfers between devices: 66.7 us -> 0.01 us  [body(): lax.all_gather(w_out, 'dp', axis=1, tiled=True)]
    unnamed x0 -> x15, local copies, waits for them, and re-layouts: none -> 15.1 us
    squeeze x0 -> x1, local copies, waits for them, and re-layouts: none -> 10.4 us  [body(): full_joined = gathered[0][0]]
  transfers between devices with their start and end apart: 16 -> 17, of which waited for: 16 -> 16; matrix products, arithmetic and copies ran while one was open for 2% -> 6% of each run, Pallas kernels for 0% -> 0%
where the time goes in v1:
time: 763 us; the launch traced here: 761 us
  waiting for transfers between devices  486 us (64%)
  matrix products  119 us (16%)
  starting transfers between devices  60.2 us (8%)
  local copies, waits for them, and re-layouts  44.6 us (6%)
  other arithmetic  25.5 us (3%)
  between operations  13.8 us (2%)
  blocking collectives  10.7 us (1%)
    ppermute x2, waiting for transfers between devices, gather_by_bits(): lax.ppermute(line, axis, [(d, (d - have) % ways) for d in range(ways)])  178 us
    ppermute x12, waiting for transfers between devices, from_behind(): lax.ppermute(value, axis, [(source, source + steps) for source in range(i...  169 us
    reduce_scatter x1, waiting for transfers between devices, body(): lax.psum_scatter(lax.dot_general(columns, rows_joined, (((0,), (0,)), (()...  81.8 us
    ppermute x12, starting transfers between devices, from_behind(): lax.ppermute(value, axis, [(source, source + steps) for source in range(i...  57.4 us
    reduce_scatter x1, waiting for transfers between devices, body(): lax.psum_scatter(lax.dot_general(columns, rows_upstream, (((0,), (0,)), (...  56.3 us
    dot_general x6, matrix products, project(): jnp.dot(normed.reshape(-1, model_width), weight, preferred_element_type=j...  35 us
    dot_general x3, matrix products, layer_backward(): lax.dot_general(grad_joined_rows.reshape(-1, grad_joined_rows.shape[2]),...  21.5 us
    dot_general x3, matrix products, layer_backward(): lax.dot_general(upstream.reshape(-1, model_width), w_out, (((1,), (1,)),...  19.8 us
  transfers between devices with their start and end apart: 17, of which 16 were waited for; matrix products, arithmetic and copies ran while one was open for 6% of the time, Pallas kernels for 0%

profile of v1, /device:TPU:0, one launch (start us, length us, event | category | flops | bytes accessed | tf_op | source)
XLA Modules:
  0.0 761.5 jit_solution(4310708183046563861)
XLA Ops:
  10.4 62.8 %collective-permute-done.2 = bf16[1,768,1664]{2,1,0:T(8,128)(2,1)S(1)} collective-permute-done((bf16[1,768,1664]{2,1,0:T(8,128)(2,1)}, bf16[1,768,1664]{2,1,0:T(8,128)(2,1)S(1)}, u32[]{:S(2)}, u32[]{:S(2)}) %collective-permute-start.2) | collective-permute-done | bytes 2555936 | tf_op jit(solution)/shard_map/ppermute | solution.py:17
  84.7 115.6 %collective-permute-done.3 = bf16[1,1536,1664]{2,1,0:T(8,128)(2,1)} collective-permute-done((bf16[1,1536,1664]{2,1,0:T(8,128)(2,1)}, bf16[1,1536,1664]{2,1,0:T(8,128)(2,1)}, u32[]{:S(2)}, u32[]{:S(2)}) %collective-permute-start.3) | collective-permute-done | bytes 5111840 | tf_op jit(solution)/shard_map/ppermute | solution.py:17
  213.8 10.4 %dynamic-slice_bitcast_fusion.2 = bf16[3072,1664]{1,0:T(8,128)(2,1)} fusion(bf16[1,6144,1664]{2,1,0:T(8,128)(2,1)} %constant_dynamic-update-slice_fusion.2, s32[]{:T(128)S(6)} %select_n.104), kind=kLoop, calls=%fused_computation.98 | loop fusion | bytes 20447236 | tf_op jit(solution)/shard_map/squeeze | solution.py:138
  224.3 122.6 %while.46 = (s32[]{:T(128)}, bf16[1,48,3072]{2,1,0:T(8,128)(2,1)S(1)}, bf16[3,1,48,3072]{3,2,1,0:T(8,128)(2,1)S(1)}, s32[]{:T(128)}, pred[]{:T(512)}, /*index=5*...) while((s32[]{:T(128)}, ...), condition=%wide.region_7.8_spmd.clone, body=%wide.region_1.7_spmd.clone.sunk | while | flops 960089920 | bytes 26255604 | solution.py:183
  224.3 14.1 %conditional.6 = (bf16[1,48,3072]{2,1,0:T(8,128)(2,1)S(1)}, bf16[3,1,48,3072]{3,2,1,0:T(8,128)(2,1)S(1)}) conditional(s32[]{:T(128)} %convert_element_type.279, bf16[3,1,48,3072]{3,2,1,0:T(8,128)(2,1)S(1)} %get-tuple-element.1143, (pred[]{:T(512)}, s32[]{:T(128)}, bf16[3,1,48,3072]{3,2,1,0:T(8,128)(2,1)}, bf16[1,48,3072]{2,1,0:T(8,128)(2,1)S(1)}, ...), branch_computations={%region_2.2_spmd, %region_3.6_spmd} | conditional | flops 960089920 | bytes 25068336 | solution.py:173
  246.5 14.1 %conditional.6 = (bf16[1,48,3072]{2,1,0:T(8,128)(2,1)S(1)}, bf16[3,1,48,3072]{3,2,1,0:T(8,128)(2,1)S(1)}) conditional(s32[]{:T(128)} %convert_element_type.279, bf16[3,1,48,3072]{3,2,1,0:T(8,128)(2,1)S(1)} %get-tuple-element.1143, (pred[]{:T(512)}, s32[]{:T(128)}, bf16[3,1,48,3072]{3,2,1,0:T(8,128)(2,1)}, bf16[1,48,3072]{2,1,0:T(8,128)(2,1)S(1)}, ...), branch_computations={%region_2.2_spmd, %region_3.6_spmd} | conditional | flops 960089920 | bytes 25068336 | solution.py:173
  270.9 14.1 %conditional.6 = (bf16[1,48,3072]{2,1,0:T(8,128)(2,1)S(1)}, bf16[3,1,48,3072]{3,2,1,0:T(8,128)(2,1)S(1)}) conditional(s32[]{:T(128)} %convert_element_type.279, bf16[3,1,48,3072]{3,2,1,0:T(8,128)(2,1)S(1)} %get-tuple-element.1143, (pred[]{:T(512)}, s32[]{:T(128)}, bf16[3,1,48,3072]{3,2,1,0:T(8,128)(2,1)}, bf16[1,48,3072]{2,1,0:T(8,128)(2,1)S(1)}, ...), branch_computations={%region_2.2_spmd, %region_3.6_spmd} | conditional | flops 960089920 | bytes 25068336 | solution.py:173
  294.5 18.4 %collective-permute-start = (bf16[1,48,3072]{2,1,0:T(8,128)(2,1)S(1)}, bf16[1,48,3072]{2,1,0:T(8,128)(2,1)S(1)}, u32[]{:S(2)}, u32[]{:S(2)}) collective-permute-start(bf16[1,48,3072]{2,1,0:T(8,128)(2,1)S(1)} %get-tuple-element.1089), channel_id=1, source_target_pairs={{0,4},{4,8},{8,12},{1,5},{5,9},{9,13},{2,6},{6,10},{10,14},{3,7},{... | collective-permute-start | bytes 884744 | tf_op jit(solution)/shard_map/while/body/eval_jaxpr/ppermute | solution.py:27
  325.9 16.8 %collective-permute-start = (bf16[1,48,3072]{2,1,0:T(8,128)(2,1)S(1)}, bf16[1,48,3072]{2,1,0:T(8,128)(2,1)S(1)}, u32[]{:S(2)}, u32[]{:S(2)}) collective-permute-start(bf16[1,48,3072]{2,1,0:T(8,128)(2,1)S(1)} %get-tuple-element.1089), channel_id=1, source_target_pairs={{0,4},{4,8},{8,12},{1,5},{5,9},{9,13},{2,6},{6,10},{10,14},{3,7},{... | collective-permute-start | bytes 884744 | tf_op jit(solution)/shard_map/while/body/eval_jaxpr/ppermute | solution.py:27
  350.5 228.9 %while.47 = (s32[]{:T(128)}, bf16[1,48,3072]{2,1,0:T(8,128)(2,1)S(1)}, bf16[3,1,48,3072]{3,2,1,0:T(8,128)(2,1)}, bf16[3,1,48,1664]{3,2,1,0:T(8,128)(2,1)}, bf16[...) while((s32[]{:T(128)}, ...), condition=%wide.region_17.18_spmd.clone, body=%wide.region_8.17_spmd.clone.sunk | while | flops 1482513152 | bytes 44631968 | solution.py:221
  352.1 7.8 %collective-permute-done.1 = bf16[1,48,3072]{2,1,0:T(8,128)(2,1)S(1)} collective-permute-done((bf16[1,48,3072]{2,1,0:T(8,128)(2,1)S(1)}, bf16[1,48,3072]{2,1,0:T(8,128)(2,1)S(1)}, u32[]{:S(2)}, u32[]{:S(2)}) %collective-permute-start.1) | collective-permute-done | bytes 294944 | tf_op jit(solution)/shard_map/while/body/eval_jaxpr/ppermute | solution.py:27
  361.3 19.9 %collective-permute-done.1 = bf16[1,48,3072]{2,1,0:T(8,128)(2,1)S(1)} collective-permute-done((bf16[1,48,3072]{2,1,0:T(8,128)(2,1)S(1)}, bf16[1,48,3072]{2,1,0:T(8,128)(2,1)S(1)}, u32[]{:S(2)}, u32[]{:S(2)}) %collective-permute-start.1) | collective-permute-done | bytes 294944 | tf_op jit(solution)/shard_map/while/body/eval_jaxpr/ppermute | solution.py:27
  382.6 88.9 %collective-permute-done.1 = bf16[1,48,3072]{2,1,0:T(8,128)(2,1)S(1)} collective-permute-done((bf16[1,48,3072]{2,1,0:T(8,128)(2,1)S(1)}, bf16[1,48,3072]{2,1,0:T(8,128)(2,1)S(1)}, u32[]{:S(2)}, u32[]{:S(2)}) %collective-permute-start.1) | collective-permute-done | bytes 294944 | tf_op jit(solution)/shard_map/while/body/eval_jaxpr/ppermute | solution.py:27
  471.5 27.3 %conditional.7 = (bf16[1,48,3072]{2,1,0:T(8,128)(2,1)S(1)}, bf16[3,1,48,3072]{3,2,1,0:T(8,128)(2,1)}, bf16[3,1,48,1664]{3,2,1,0:T(8,128)(2,1)}, bf16[3,1,48,1536...) conditional(s32[]{:T(128)} %convert_element_type.280, ...), branch_computations={%region_9.9_spmd, %region_10.16_spmd} | conditional | flops 1482513152 | bytes 43444584 | solution.py:210
  500.1 7.3 collective-permute-done.1
  507.5 27.3 %conditional.7 = (bf16[1,48,3072]{2,1,0:T(8,128)(2,1)S(1)}, bf16[3,1,48,3072]{3,2,1,0:T(8,128)(2,1)}, bf16[3,1,48,1664]{3,2,1,0:T(8,128)(2,1)}, bf16[3,1,48,1536...) conditional(s32[]{:T(128)} %convert_element_type.280, ...), branch_computations={%region_9.9_spmd, %region_10.16_spmd} | conditional | flops 1482513152 | bytes 43444584 | solution.py:210
  536.1 7.4 collective-permute-done.1
  543.5 27.3 %conditional.7 = (bf16[1,48,3072]{2,1,0:T(8,128)(2,1)S(1)}, bf16[3,1,48,3072]{3,2,1,0:T(8,128)(2,1)}, bf16[3,1,48,1664]{3,2,1,0:T(8,128)(2,1)}, bf16[3,1,48,1536...) conditional(s32[]{:T(128)} %convert_element_type.280, ...), branch_computations={%region_9.9_spmd, %region_10.16_spmd} | conditional | flops 1482513152 | bytes 43444584 | solution.py:210
  572.1 7.3 collective-permute-done.1
  579.4 7.6 %bitcast_convert_fusion.1 = bf16[1536,3072]{1,0:T(8,128)(2,1)} fusion(bf16[3,1,48,3072]{3,2,1,0:T(8,128)(2,1)} %get-tuple-element.812, bf16[3,1,48,1536]{3,2,1,0:T(8,128)(2,1)} %get-tuple-element.811), kind=kOutput, calls=%fused_computation.97 | convolution fusion | flops 1363673088 | bytes 10764288 | tf_op jit(solution)/shard_map/dot_general | solution.py:237
  587.4 9.9 %bitcast_convert_fusion = bf16[3072,1664]{1,0:T(8,128)(2,1)} fusion(bf16[3,1,48,3072]{3,2,1,0:T(8,128)(2,1)} %get-tuple-element.809, bf16[3,1,48,1664]{3,2,1,0:T(8,128)(2,1)} %get-tuple-element.810), kind=kOutput, calls=%fused_computation.96 | convolution fusion | flops 1477312512 | bytes 11587584 | tf_op jit(solution)/shard_map/dot_general | solution.py:228
  597.3 10.7 %psum.7 = f32[1,3072]{1,0:T(1,128)} all-reduce(f32[1,3072]{1,0:T(1,128)S(1)} %bitcast.206), channel_id=1, replica_groups=mesh['groups'=2,'section'=4,'dp'=4] {'dp'}, use_global_device_ids=true, to_apply=%region_20.21 | all-reduce | flops 3072 | bytes 24576 | tf_op jit(solution)/shard_map/psum | solution.py:244
  608.0 56.3 %reduce-scatter.5.cloned.1.call-done = bf16[384,3072]{1,0:T(8,128)(2,1)} async-done(((bf16[1536,3072]{1,0:T(8,128)(2,1)}), bf16[384,3072]{1,0:T(8,128)(2,1)}) %reduce-scatter.5.cloned.1.call-update) | async-done | bytes 2359312 | tf_op jit(solution)/shard_map/reduce_scatter | solution.py:236
  668.8 81.8 %reduce-scatter.3.cloned.1.call-done = bf16[768,1664]{1,0:T(8,128)(2,1)} async-done(((bf16[3072,1664]{1,0:T(8,128)(2,1)}), bf16[768,1664]{1,0:T(8,128)(2,1)}) %reduce-scatter.3.cloned.1.call-update) | async-done | bytes 2555920 | tf_op jit(solution)/shard_map/reduce_scatter | solution.py:227
  (209 shorter events, 217.5 us)
Async XLA Ops:
  7.2 72.3 %copy-start = (bf16[1,768,1664]{2,1,0:T(8,128)(2,1)S(1)}, bf16[1,768,1664]{2,1,0:T(8,128)(2,1)}, u32[]{:S(2)}) copy-start(bf16[1,768,1664]{2,1,0:T(8,128)(2,1)} %param.18) | copy-start | bytes 7667716
  7.2 71.9 %copy-start.4 = (s32[3,3,3]{2,1,0:T(4,128)S(1)}, s32[3,3,3]{2,1,0:T(4,128)}, u32[]{:S(2)}) copy-start(s32[3,3,3]{2,1,0:T(4,128)} %param.16) | copy-start | bytes 328
  7.2 217.0 %all-gather.2.cloned.1.call-start = ((), (), s32[]{:S(2)}) async-start(), calls=%async_computation.2 | async-start | bytes 11796480 | tf_op jit(solution)/shard_map/all_gather | solution.py:137
  7.9 656.4 %reduce-scatter.5.cloned.1.call-start = ((), (), s32[]{:S(2)}) async-start(), calls=%async_computation.4 | async-start | bytes 11796480 | tf_op jit(solution)/shard_map/reduce_scatter | solution.py:236
  8.0 65.2 %collective-permute-start.2 = (bf16[1,768,1664]{2,1,0:T(8,128)(2,1)}, bf16[1,768,1664]{2,1,0:T(8,128)(2,1)S(1)}, u32[]{:S(2)}, u32[]{:S(2)}) collective-permute-start(bf16[1,768,1664]{2,1,0:T(8,128)(2,1)} %param.18), channel_id=1, source_target_pairs={{0,3},{1,0},{2,1},{3,2},{4,7},{5,4},{6,5},{7,6},{8,11},{9,8},{10,9... | collective-permute-start | bytes 7667720 | tf_op jit(solution)/shard_map/ppermute | solution.py:17
  73.2 1.5 copy-start.1
  79.1 121.2 %collective-permute-start.3 = (bf16[1,1536,1664]{2,1,0:T(8,128)(2,1)}, bf16[1,1536,1664]{2,1,0:T(8,128)(2,1)}, u32[]{:S(2)}, u32[]{:S(2)}) collective-permute-start(bf16[1,1536,1664]{2,1,0:T(8,128)(2,1)} %pad_maximum_fusion), channel_id=1, source_target_pairs={{0,2},{1,3},{2,0},{3,1},{4,6},{5,7},{6,4},{7,5},{8,10},{9,11},{10,... | collective-permute-start | bytes 15335432 | tf_op jit(solution)/shard_map/ppermute | solution.py:17
  81.1 125.9 %copy-start.2 = (bf16[1,768,1664]{2,1,0:T(8,128)(2,1)S(1)}, bf16[1,768,1664]{2,1,0:T(8,128)(2,1)}, u32[]{:S(2)}) copy-start(bf16[1,768,1664]{2,1,0:T(8,128)(2,1)} %copy-done.1) | copy-start | bytes 7667716
  213.8 10.5 %copy-start.3 = (f32[1,3072]{1,0:T(1,128)S(1)}, f32[1,3072]{1,0:T(1,128)}, u32[]{:S(2)}) copy-start(f32[1,3072]{1,0:T(1,128)} %param.17) | copy-start | bytes 36868
  238.4 8.1 %collective-permute-start = (bf16[1,48,3072]{2,1,0:T(8,128)(2,1)S(1)}, bf16[1,48,3072]{2,1,0:T(8,128)(2,1)S(1)}, u32[]{:S(2)}, u32[]{:S(2)}) collective-permute-start(bf16[1,48,3072]{2,1,0:T(8,128)(2,1)S(1)} %get-tuple-element.1089), channel_id=1, source_target_pairs={{0,4},{4,8},{8,12},{1,5},{5,9},{9,13},{2,6},{6,10},{10,14},{3,7},{... | collective-permute-start | bytes 884744 | tf_op jit(solution)/shard_map/while/body/eval_jaxpr/ppermute | solution.py:27
  260.5 10.4 %collective-permute-start = (bf16[1,48,3072]{2,1,0:T(8,128)(2,1)S(1)}, bf16[1,48,3072]{2,1,0:T(8,128)(2,1)S(1)}, u32[]{:S(2)}, u32[]{:S(2)}) collective-permute-start(bf16[1,48,3072]{2,1,0:T(8,128)(2,1)S(1)} %get-tuple-element.1089), channel_id=1, source_target_pairs={{0,4},{4,8},{8,12},{1,5},{5,9},{9,13},{2,6},{6,10},{10,14},{3,7},{... | collective-permute-start | bytes 884744 | tf_op jit(solution)/shard_map/while/body/eval_jaxpr/ppermute | solution.py:27
  285.0 9.5 %collective-permute-start = (bf16[1,48,3072]{2,1,0:T(8,128)(2,1)S(1)}, bf16[1,48,3072]{2,1,0:T(8,128)(2,1)S(1)}, u32[]{:S(2)}, u32[]{:S(2)}) collective-permute-start(bf16[1,48,3072]{2,1,0:T(8,128)(2,1)S(1)} %get-tuple-element.1089), channel_id=1, source_target_pairs={{0,4},{4,8},{8,12},{1,5},{5,9},{9,13},{2,6},{6,10},{10,14},{3,7},{... | collective-permute-start | bytes 884744 | tf_op jit(solution)/shard_map/while/body/eval_jaxpr/ppermute | solution.py:27
  294.5 22.6 %collective-permute-start = (bf16[1,48,3072]{2,1,0:T(8,128)(2,1)S(1)}, bf16[1,48,3072]{2,1,0:T(8,128)(2,1)S(1)}, u32[]{:S(2)}, u32[]{:S(2)}) collective-permute-start(bf16[1,48,3072]{2,1,0:T(8,128)(2,1)S(1)} %get-tuple-element.1089), channel_id=1, source_target_pairs={{0,4},{4,8},{8,12},{1,5},{5,9},{9,13},{2,6},{6,10},{10,14},{3,7},{... | collective-permute-start | bytes 884744 | tf_op jit(solution)/shard_map/while/body/eval_jaxpr/ppermute | solution.py:27
  317.2 8.6 %collective-permute-start = (bf16[1,48,3072]{2,1,0:T(8,128)(2,1)S(1)}, bf16[1,48,3072]{2,1,0:T(8,128)(2,1)S(1)}, u32[]{:S(2)}, u32[]{:S(2)}) collective-permute-start(bf16[1,48,3072]{2,1,0:T(8,128)(2,1)S(1)} %get-tuple-element.1089), channel_id=1, source_target_pairs={{0,4},{4,8},{8,12},{1,5},{5,9},{9,13},{2,6},{6,10},{10,14},{3,7},{... | collective-permute-start | bytes 884744 | tf_op jit(solution)/shard_map/while/body/eval_jaxpr/ppermute | solution.py:27
  325.9 21.0 %collective-permute-start = (bf16[1,48,3072]{2,1,0:T(8,128)(2,1)S(1)}, bf16[1,48,3072]{2,1,0:T(8,128)(2,1)S(1)}, u32[]{:S(2)}, u32[]{:S(2)}) collective-permute-start(bf16[1,48,3072]{2,1,0:T(8,128)(2,1)S(1)} %get-tuple-element.1089), channel_id=1, source_target_pairs={{0,4},{4,8},{8,12},{1,5},{5,9},{9,13},{2,6},{6,10},{10,14},{3,7},{... | collective-permute-start | bytes 884744 | tf_op jit(solution)/shard_map/while/body/eval_jaxpr/ppermute | solution.py:27
  350.8 9.1 %collective-permute-start.1 = (bf16[1,48,3072]{2,1,0:T(8,128)(2,1)S(1)}, bf16[1,48,3072]{2,1,0:T(8,128)(2,1)S(1)}, u32[]{:S(2)}, u32[]{:S(2)}) collective-permute-start(bf16[1,48,3072]{2,1,0:T(8,128)(2,1)S(1)} %get-tuple-element.1106), channel_id=1, source_target_pairs={{4,0},{8,4},{12,8},{5,1},{9,5},{13,9},{6,2},{10,6},{14,10},{7,3},{... | collective-permute-start | bytes 884744 | tf_op jit(solution)/shard_map/while/body/eval_jaxpr/ppermute | solution.py:27
  360.0 21.2 %collective-permute-start.1 = (bf16[1,48,3072]{2,1,0:T(8,128)(2,1)S(1)}, bf16[1,48,3072]{2,1,0:T(8,128)(2,1)S(1)}, u32[]{:S(2)}, u32[]{:S(2)}) collective-permute-start(bf16[1,48,3072]{2,1,0:T(8,128)(2,1)S(1)} %get-tuple-element.1106), channel_id=1, source_target_pairs={{4,0},{8,4},{12,8},{5,1},{9,5},{13,9},{6,2},{10,6},{14,10},{7,3},{... | collective-permute-start | bytes 884744 | tf_op jit(solution)/shard_map/while/body/eval_jaxpr/ppermute | solution.py:27
  381.2 90.2 %collective-permute-start.1 = (bf16[1,48,3072]{2,1,0:T(8,128)(2,1)S(1)}, bf16[1,48,3072]{2,1,0:T(8,128)(2,1)S(1)}, u32[]{:S(2)}, u32[]{:S(2)}) collective-permute-start(bf16[1,48,3072]{2,1,0:T(8,128)(2,1)S(1)} %get-tuple-element.1106), channel_id=1, source_target_pairs={{4,0},{8,4},{12,8},{5,1},{9,5},{13,9},{6,2},{10,6},{14,10},{7,3},{... | collective-permute-start | bytes 884744 | tf_op jit(solution)/shard_map/while/body/eval_jaxpr/ppermute | solution.py:27
  498.8 8.6 %collective-permute-start.1 = (bf16[1,48,3072]{2,1,0:T(8,128)(2,1)S(1)}, bf16[1,48,3072]{2,1,0:T(8,128)(2,1)S(1)}, u32[]{:S(2)}, u32[]{:S(2)}) collective-permute-start(bf16[1,48,3072]{2,1,0:T(8,128)(2,1)S(1)} %get-tuple-element.1106), channel_id=1, source_target_pairs={{4,0},{8,4},{12,8},{5,1},{9,5},{13,9},{6,2},{10,6},{14,10},{7,3},{... | collective-permute-start | bytes 884744 | tf_op jit(solution)/shard_map/while/body/eval_jaxpr/ppermute | solution.py:27
  534.8 8.7 %collective-permute-start.1 = (bf16[1,48,3072]{2,1,0:T(8,128)(2,1)S(1)}, bf16[1,48,3072]{2,1,0:T(8,128)(2,1)S(1)}, u32[]{:S(2)}, u32[]{:S(2)}) collective-permute-start(bf16[1,48,3072]{2,1,0:T(8,128)(2,1)S(1)} %get-tuple-element.1106), channel_id=1, source_target_pairs={{4,0},{8,4},{12,8},{5,1},{9,5},{13,9},{6,2},{10,6},{14,10},{7,3},{... | collective-permute-start | bytes 884744 | tf_op jit(solution)/shard_map/while/body/eval_jaxpr/ppermute | solution.py:27
  570.8 8.6 %collective-permute-start.1 = (bf16[1,48,3072]{2,1,0:T(8,128)(2,1)S(1)}, bf16[1,48,3072]{2,1,0:T(8,128)(2,1)S(1)}, u32[]{:S(2)}, u32[]{:S(2)}) collective-permute-start(bf16[1,48,3072]{2,1,0:T(8,128)(2,1)S(1)} %get-tuple-element.1106), channel_id=1, source_target_pairs={{4,0},{8,4},{12,8},{5,1},{9,5},{13,9},{6,2},{10,6},{14,10},{7,3},{... | collective-permute-start | bytes 884744 | tf_op jit(solution)/shard_map/while/body/eval_jaxpr/ppermute | solution.py:27
  587.1 163.5 %reduce-scatter.3.cloned.1.call-start = ((), (), s32[]{:S(2)}) async-start(), calls=%async_computation.3 | async-start | bytes 12779520 | tf_op jit(solution)/shard_map/reduce_scatter | solution.py:227
Sparse Core Ops, SparseCore 0:
  9.6 90.7 all-gather.1
  587.2 77.0 reduce-scatter.4
  667.0 83.5 reduce-scatter.2
